TPU v7x, 32 devices: a whole 2x2x4 slice. The times are simulated.
32 devices in a mesh: dp: 4 (over y, x), fsdp: 8 (over z, core).
Axes of the slice: x: 2, y: 2, z: 4, core: 2. Of those that a mesh axis runs over, the one named last changes fastest.
Arguments:
- tokens: bfloat16 [32, 512, 768], P(('dp', 'fsdp')), may hold values from -6 to 6
- lengths: int32 [32], P(('dp', 'fsdp')), may hold values from 30 to 512, as said below
- cotangent: bfloat16 [32, 512, 768], P(('dp', 'fsdp')), may hold values from -6 to 6
- query_weight: bfloat16 [768, 768], P('fsdp'), may hold values from -0.21875 to 0.21875
- query_bias: bfloat16 [768], P('fsdp'), may hold values from -3 to 3
- key_weight: bfloat16 [768, 768], P('fsdp'), may hold values from -0.21875 to 0.21875
- value_weight: bfloat16 [768, 768], P('fsdp'), may hold values from -0.21875 to 0.21875
- value_bias: bfloat16 [768], P('fsdp'), may hold values from -3 to 3
- output_weight: bfloat16 [768, 768], P('fsdp'), may hold values from -3.5 to 3.5
- output_bias: bfloat16 [768], P('fsdp'), may hold values from -3 to 3
- first_gain: bfloat16 [768], P('fsdp'), may hold values from 0.25 to 1.75
- first_shift: bfloat16 [768], P('fsdp'), may hold values from -3 to 3
- inner_weight: bfloat16 [768, 3072], P('fsdp'), may hold values from -0.21875 to 0.21875
- inner_bias: bfloat16 [3072], P('fsdp'), may hold values from -3 to 3
- outer_weight: bfloat16 [3072, 768], P('fsdp'), may hold values from -0.109375 to 0.109375
- outer_bias: bfloat16 [768], P('fsdp'), may hold values from -3 to 3
- second_gain: bfloat16 [768], P('fsdp'), may hold values from 0.25 to 1.75
- second_shift: bfloat16 [768], P('fsdp'), may hold values from -3 to 3
Outputs:
- block_output: bfloat16 [32, 512, 768], P(('dp', 'fsdp'))
- input_grad: float32 [32, 512, 768], P(('dp', 'fsdp'))
- query_weight_grad: float32 [768, 768], P('fsdp')
- query_bias_grad: float32 [768], P('fsdp')
- key_weight_grad: float32 [768, 768], P('fsdp')
- value_weight_grad: float32 [768, 768], P('fsdp')
- value_bias_grad: float32 [768], P('fsdp')
- output_weight_grad: float32 [768, 768], P('fsdp')
- output_bias_grad: float32 [768], P('fsdp')
- first_gain_grad: float32 [768], P('fsdp')
- first_shift_grad: float32 [768], P('fsdp')
- inner_weight_grad: float32 [768, 3072], P('fsdp')
- inner_bias_grad: float32 [3072], P('fsdp')
- outer_weight_grad: float32 [3072, 768], P('fsdp')
- outer_bias_grad: float32 [768], P('fsdp')
- second_gain_grad: float32 [768], P('fsdp')
- second_shift_grad: float32 [768], P('fsdp')
Inputs may be any that keep to these rules, and one draw needn't show every extreme that they name: Document i holds its true tokens in slots 0 to lengths[i] - 1, the rest is padding; in every draw some document has exactly 512 and another exactly 30.
All inputs are finite; a program needn't handle non-finite values.
Results may differ from a plain program's by a relative error of at most 0.015.
Values may be sent and summed in bfloat16 or wider, within the bound.
No kernel may reach another device: no remote copies, remote signals or barrier semaphores. Data moves between devices by JAX's collectives and lax.ppermute only.
A program may use at most 192 MiB of HBM per device.

v0:
```python
import math
import jax
import jax.numpy as jnp
from jax import lax
from jax.sharding import PartitionSpec as P

HD = 64
epsilon = 1e-12
masked_score = -1e30
root_half = math.sqrt(0.5)
inv_root_two_pi = 1.0 / math.sqrt(2.0 * math.pi)


def normalize(values):
    center = values - jnp.mean(values, axis=-1, keepdims=True)
    scaled = lax.rsqrt(jnp.mean(center * center, axis=-1, keepdims=True) + epsilon)
    return (center * scaled, scaled)


def norm_back(grad_in, normed, scaled):
    first_mean = jnp.mean(grad_in, axis=-1, keepdims=True)
    second_mean = jnp.mean(grad_in * normed, axis=-1, keepdims=True)
    return scaled * (grad_in - first_mean - normed * second_mean)


def gelu_parts(inner):
    cumulative = 0.5 * (1.0 + lax.erf(inner * root_half))
    density = jnp.exp(-0.5 * inner * inner) * inv_root_two_pi
    return (inner * cumulative, cumulative + inner * density)


def score_block(queries, keysets, length):
    seq_len = queries.shape[0]
    scores = jnp.einsum(
        "qhd,khd->hqk", queries, keysets, preferred_element_type=jnp.float32
    ) * queries.shape[2] ** (-0.5)
    allowed = jnp.arange(seq_len, dtype=jnp.int32) < length
    return jnp.where(allowed[None, None, :], scores, masked_score)


def attend_forward(pieces):
    queries, keysets, values, length = pieces
    scores = score_block(queries, keysets, length)
    highest = jnp.max(scores, axis=-1, keepdims=True)
    logsum = highest + jnp.log(jnp.sum(jnp.exp(scores - highest), axis=-1, keepdims=True))
    probs = jnp.exp(scores - logsum).astype(jnp.bfloat16)
    attended = jnp.einsum("hqk,khd->qhd", probs, values, preferred_element_type=jnp.float32)
    return (attended.astype(jnp.bfloat16), logsum)


def attend_backward(pieces):
    queries, keysets, values, length, logsum, attended_grad = pieces
    scale = queries.shape[2] ** (-0.5)
    scores = score_block(queries, keysets, length)
    probs_full = jnp.exp(scores - logsum)
    probs = probs_full.astype(jnp.bfloat16)
    values_grad = jnp.einsum(
        "hqk,qhd->khd", probs, attended_grad, preferred_element_type=jnp.float32
    )
    prob_grad = jnp.einsum(
        "qhd,khd->hqk", attended_grad, values, preferred_element_type=jnp.float32
    )
    row_term = jnp.sum(prob_grad * probs_full, axis=-1, keepdims=True)
    score_grad = (probs_full * (prob_grad - row_term)).astype(jnp.bfloat16)
    queries_grad = (
        jnp.einsum("hqk,khd->qhd", score_grad, keysets, preferred_element_type=jnp.float32) * scale
    )
    keys_grad = (
        jnp.einsum("hqk,qhd->khd", score_grad, queries, preferred_element_type=jnp.float32) * scale
    )
    return (
        queries_grad.astype(jnp.bfloat16),
        keys_grad.astype(jnp.bfloat16),
        values_grad.astype(jnp.bfloat16),
    )


def column_sum(values):
    return jnp.sum(values.astype(jnp.float32), axis=0)


def weight_grad(left, right):
    return jnp.einsum("tr,tc->rc", left, right, preferred_element_type=jnp.float32)


def back_product(grad_rows, weights):
    return jnp.einsum("tc,rc->tr", grad_rows, weights, preferred_element_type=jnp.float32)


def on_device(
    tokens,
    lengths,
    cotangent,
    query_weight,
    query_bias,
    key_weight,
    value_weight,
    value_bias,
    output_weight,
    output_bias,
    first_gain,
    first_shift,
    inner_weight,
    inner_bias,
    outer_weight,
    outer_bias,
    second_gain,
    second_shift,
):
    gathered = (
        lax.all_gather(query_weight, "fsdp", axis=0, tiled=True),
        lax.all_gather(query_bias, "fsdp", axis=0, tiled=True),
        lax.all_gather(key_weight, "fsdp", axis=0, tiled=True),
        lax.all_gather(value_weight, "fsdp", axis=0, tiled=True),
        lax.all_gather(value_bias, "fsdp", axis=0, tiled=True),
        lax.all_gather(output_weight, "fsdp", axis=0, tiled=True),
        lax.all_gather(output_bias, "fsdp", axis=0, tiled=True),
        lax.all_gather(first_gain, "fsdp", axis=0, tiled=True),
        lax.all_gather(first_shift, "fsdp", axis=0, tiled=True),
        lax.all_gather(inner_weight, "fsdp", axis=0, tiled=True),
        lax.all_gather(inner_bias, "fsdp", axis=0, tiled=True),
        lax.all_gather(outer_weight, "fsdp", axis=0, tiled=True),
        lax.all_gather(outer_bias, "fsdp", axis=0, tiled=True),
        lax.all_gather(second_gain, "fsdp", axis=0, tiled=True),
        lax.all_gather(second_shift, "fsdp", axis=0, tiled=True),
    )
    (
        full_query,
        full_qbias,
        full_key,
        full_value,
        full_vbias,
        full_output,
        full_obias,
        full_gain_one,
        full_shift_one,
        full_inner,
        full_ibias,
        full_outer,
        full_ubias,
        full_gain_two,
        full_shift_two,
    ) = gathered
    doc_count, seq_len, width = tokens.shape
    row_count = doc_count * seq_len
    heads = width // HD
    flat_in = tokens.reshape(row_count, width)
    queries = (
        jnp.dot(flat_in, full_query, preferred_element_type=jnp.float32)
        + full_qbias.astype(jnp.float32)
    ).astype(jnp.bfloat16)
    keysets = jnp.dot(flat_in, full_key, preferred_element_type=jnp.float32).astype(jnp.bfloat16)
    values = (
        jnp.dot(flat_in, full_value, preferred_element_type=jnp.float32)
        + full_vbias.astype(jnp.float32)
    ).astype(jnp.bfloat16)
    shaped = (doc_count, seq_len, heads, HD)
    query_docs = queries.reshape(shaped)
    key_docs = keysets.reshape(shaped)
    value_docs = values.reshape(shaped)
    attended, logsum = lax.map(attend_forward, (query_docs, key_docs, value_docs, lengths))
    attended = attended.reshape(row_count, width)
    first_sum = (
        flat_in.astype(jnp.float32)
        + jnp.dot(attended, full_output, preferred_element_type=jnp.float32)
        + full_obias.astype(jnp.float32)
    )
    normed_one, rstd_one = normalize(first_sum)
    hidden = normed_one * full_gain_one.astype(jnp.float32) + full_shift_one.astype(jnp.float32)
    hidden_low = hidden.astype(jnp.bfloat16)
    inner = jnp.dot(hidden_low, full_inner, preferred_element_type=jnp.float32) + full_ibias.astype(
        jnp.float32
    )
    activated_full, slope = gelu_parts(inner)
    activated = activated_full.astype(jnp.bfloat16)
    second_sum = (
        hidden
        + jnp.dot(activated, full_outer, preferred_element_type=jnp.float32)
        + full_ubias.astype(jnp.float32)
    )
    normed_two, rstd_two = normalize(second_sum)
    valid = (
        (jnp.arange(seq_len, dtype=jnp.int32)[None, :] < lengths[:, None])
        .astype(jnp.float32)
        .reshape(row_count, 1)
    )
    result = valid * (
        normed_two * full_gain_two.astype(jnp.float32) + full_shift_two.astype(jnp.float32)
    )
    block_output = result.astype(jnp.bfloat16).reshape(doc_count, seq_len, width)
    again = (
        lax.all_gather(query_weight, "fsdp", axis=0, tiled=True),
        lax.all_gather(query_bias, "fsdp", axis=0, tiled=True),
        lax.all_gather(key_weight, "fsdp", axis=0, tiled=True),
        lax.all_gather(value_weight, "fsdp", axis=0, tiled=True),
        lax.all_gather(value_bias, "fsdp", axis=0, tiled=True),
        lax.all_gather(output_weight, "fsdp", axis=0, tiled=True),
        lax.all_gather(output_bias, "fsdp", axis=0, tiled=True),
        lax.all_gather(first_gain, "fsdp", axis=0, tiled=True),
        lax.all_gather(first_shift, "fsdp", axis=0, tiled=True),
        lax.all_gather(inner_weight, "fsdp", axis=0, tiled=True),
        lax.all_gather(inner_bias, "fsdp", axis=0, tiled=True),
        lax.all_gather(outer_weight, "fsdp", axis=0, tiled=True),
        lax.all_gather(outer_bias, "fsdp", axis=0, tiled=True),
        lax.all_gather(second_gain, "fsdp", axis=0, tiled=True),
        lax.all_gather(second_shift, "fsdp", axis=0, tiled=True),
    )
    back_query = again[0]
    back_key = again[2]
    back_value = again[3]
    back_output = again[5]
    back_gain_one = again[7]
    back_inner = again[9]
    back_outer = again[11]
    back_gain_two = again[13]
    out_grad = cotangent.reshape(row_count, width).astype(jnp.float32) * valid
    second_shift_grad = jnp.sum(out_grad, axis=0)
    second_gain_grad = jnp.sum(out_grad * normed_two, axis=0)
    second_sum_grad = norm_back(out_grad * back_gain_two.astype(jnp.float32), normed_two, rstd_two)
    outer_grad_low = second_sum_grad.astype(jnp.bfloat16)
    outer_bias_grad = column_sum(outer_grad_low)
    outer_weight_grad = weight_grad(activated, outer_grad_low)
    inner_grad_low = (back_product(outer_grad_low, back_outer) * slope).astype(jnp.bfloat16)
    inner_bias_grad = column_sum(inner_grad_low)
    inner_weight_grad = weight_grad(hidden_low, inner_grad_low)
    hidden_grad = back_product(inner_grad_low, back_inner) + second_sum_grad
    first_shift_grad = jnp.sum(hidden_grad, axis=0)
    first_gain_grad = jnp.sum(hidden_grad * normed_one, axis=0)
    first_sum_grad = norm_back(
        hidden_grad * back_gain_one.astype(jnp.float32), normed_one, rstd_one
    )
    branch_grad_low = first_sum_grad.astype(jnp.bfloat16)
    output_bias_grad = column_sum(branch_grad_low)
    output_weight_grad = weight_grad(attended, branch_grad_low)
    attended_grad_low = back_product(branch_grad_low, back_output).astype(jnp.bfloat16)
    queries_grad, keys_grad, values_grad = lax.map(
        attend_backward,
        (query_docs, key_docs, value_docs, lengths, logsum, attended_grad_low.reshape(shaped)),
    )
    queries_grad = queries_grad.reshape(row_count, width)
    keys_grad = keys_grad.reshape(row_count, width)
    values_grad = values_grad.reshape(row_count, width)
    query_bias_grad = column_sum(queries_grad)
    value_bias_grad = column_sum(values_grad)
    query_weight_grad = weight_grad(flat_in, queries_grad)
    key_weight_grad = weight_grad(flat_in, keys_grad)
    value_weight_grad = weight_grad(flat_in, values_grad)
    input_grad = (
        first_sum_grad
        + back_product(queries_grad, back_query)
        + back_product(keys_grad, back_key)
        + back_product(values_grad, back_value)
    )
    local_grads = (
        query_weight_grad,
        query_bias_grad,
        key_weight_grad,
        value_weight_grad,
        value_bias_grad,
        output_weight_grad,
        output_bias_grad,
        first_gain_grad,
        first_shift_grad,
        inner_weight_grad,
        inner_bias_grad,
        outer_weight_grad,
        outer_bias_grad,
        second_gain_grad,
        second_shift_grad,
    )
    owned = (
        lax.psum_scatter(local_grads[0], "fsdp", scatter_dimension=0, tiled=True),
        lax.psum_scatter(local_grads[1], "fsdp", scatter_dimension=0, tiled=True),
        lax.psum_scatter(local_grads[2], "fsdp", scatter_dimension=0, tiled=True),
        lax.psum_scatter(local_grads[3], "fsdp", scatter_dimension=0, tiled=True),
        lax.psum_scatter(local_grads[4], "fsdp", scatter_dimension=0, tiled=True),
        lax.psum_scatter(local_grads[5], "fsdp", scatter_dimension=0, tiled=True),
        lax.psum_scatter(local_grads[6], "fsdp", scatter_dimension=0, tiled=True),
        lax.psum_scatter(local_grads[7], "fsdp", scatter_dimension=0, tiled=True),
        lax.psum_scatter(local_grads[8], "fsdp", scatter_dimension=0, tiled=True),
        lax.psum_scatter(local_grads[9], "fsdp", scatter_dimension=0, tiled=True),
        lax.psum_scatter(local_grads[10], "fsdp", scatter_dimension=0, tiled=True),
        lax.psum_scatter(local_grads[11], "fsdp", scatter_dimension=0, tiled=True),
        lax.psum_scatter(local_grads[12], "fsdp", scatter_dimension=0, tiled=True),
        lax.psum_scatter(local_grads[13], "fsdp", scatter_dimension=0, tiled=True),
        lax.psum_scatter(local_grads[14], "fsdp", scatter_dimension=0, tiled=True),
    )
    summed = (
        lax.psum(owned[0].astype(jnp.bfloat16), "dp").astype(jnp.float32),
        lax.psum(owned[1].astype(jnp.bfloat16), "dp").astype(jnp.float32),
        lax.psum(owned[2].astype(jnp.bfloat16), "dp").astype(jnp.float32),
        lax.psum(owned[3].astype(jnp.bfloat16), "dp").astype(jnp.float32),
        lax.psum(owned[4].astype(jnp.bfloat16), "dp").astype(jnp.float32),
        lax.psum(owned[5].astype(jnp.bfloat16), "dp").astype(jnp.float32),
        lax.psum(owned[6].astype(jnp.bfloat16), "dp").astype(jnp.float32),
        lax.psum(owned[7].astype(jnp.bfloat16), "dp").astype(jnp.float32),
        lax.psum(owned[8].astype(jnp.bfloat16), "dp").astype(jnp.float32),
        lax.psum(owned[9].astype(jnp.bfloat16), "dp").astype(jnp.float32),
        lax.psum(owned[10].astype(jnp.bfloat16), "dp").astype(jnp.float32),
        lax.psum(owned[11].astype(jnp.bfloat16), "dp").astype(jnp.float32),
        lax.psum(owned[12].astype(jnp.bfloat16), "dp").astype(jnp.float32),
        lax.psum(owned[13].astype(jnp.bfloat16), "dp").astype(jnp.float32),
        lax.psum(owned[14].astype(jnp.bfloat16), "dp").astype(jnp.float32),
    )
    return (
        block_output,
        input_grad.reshape(doc_count, seq_len, width),
        summed[0],
        summed[1],
        summed[2],
        summed[3],
        summed[4],
        summed[5],
        summed[6],
        summed[7],
        summed[8],
        summed[9],
        summed[10],
        summed[11],
        summed[12],
        summed[13],
        summed[14],
    )


def solution(mesh):
    in_specs = (
        P(("dp", "fsdp"), None, None),
        P(("dp", "fsdp")),
        P(("dp", "fsdp"), None, None),
        P("fsdp", None),
        P("fsdp"),
        P("fsdp", None),
        P("fsdp", None),
        P("fsdp"),
        P("fsdp", None),
        P("fsdp"),
        P("fsdp"),
        P("fsdp"),
        P("fsdp", None),
        P("fsdp"),
        P("fsdp", None),
        P("fsdp"),
        P("fsdp"),
        P("fsdp"),
    )
    out_specs = (
        P(("dp", "fsdp"), None, None),
        P(("dp", "fsdp"), None, None),
        P("fsdp", None),
        P("fsdp"),
        P("fsdp", None),
        P("fsdp", None),
        P("fsdp"),
        P("fsdp", None),
        P("fsdp"),
        P("fsdp"),
        P("fsdp"),
        P("fsdp", None),
        P("fsdp"),
        P("fsdp", None),
        P("fsdp"),
        P("fsdp"),
        P("fsdp"),
    )
    return jax.shard_map(
        on_device, mesh=mesh, in_specs=in_specs, out_specs=out_specs, check_vma=False
    )
```

profile of v0, /device:TPU:0, one launch (start us, length us, event | category | flops | bytes accessed | tf_op | source)
XLA Modules:
  0.0 681.5 jit_solution(11375898888319952286)
XLA Ops:
  14.5 30.3 %all-reduce.18 = (bf16[768]{0:T(1024)(128)(2,1)S(1)}, bf16[768]{0:T(1024)(128)(2,1)S(1)}, bf16[768]{0:T(1024)(128)(2,1)S(1)}, bf16[768]{0:T(1024)(128)(2,1)S(1)}...) all-reduce(bf16[768]{0:T(1024)(128)(2,1)S(1)} %dynamic-update-slice, ...), channel_id=1, replica_groups=mesh['dp'=4,'fsdp'=8] {'fsdp'}, use_global_device_ids=true, to_apply=%add | all-reduce | flops 6144 | bytes 24576
  45.5 13.0 %all-gather = bf16[8,1,384]{2,1,0:T(2,128)(2,1)S(1)} all-gather(bf16[1,1,384]{2,1,0:T(2,128)(2,1)S(1)} %reshape.181), channel_id=1, replica_groups=mesh['dp'=4,'fsdp'=8] {'fsdp'}, dimensions={0}, use_global_device_ids=true | all-gather | bytes 6912 | tf_op jit(solution)/shard_map/all_gather | solution.py:121
  63.6 19.9 %all-gather.8.cloned.1.call-done = bf16[768,768]{1,0:T(8,128)(2,1)} async-done(((bf16[96,768]{1,0:T(8,128)(2,1)}), bf16[768,768]{1,0:T(8,128)(2,1)}) %all-gather.8.cloned.1.call-update) | async-done | bytes 1179664 | tf_op jit(solution)/shard_map/all_gather | solution.py:114
  83.5 2.9 add_convert_fusion.1
  87.8 3.1 fusion
  90.9 2.6 exponential_reduce_fusion
  95.5 9.9 %fusion.1 = bf16[12,512,512]{1,2,0:T(8,128)(2,1)} fusion(f32[12,512,512]{1,2,0:T(8,128)} %copy-done, f32[12,512]{1,0:T(8,128)S(1)} %log_add_fusion, pred[512]{0:T(512)(128)(4,1)S(1)} %iota_compare_fusion), kind=kLoop, calls=%fused_computation.7 | loop fusion | flops 12582912 | bytes 18899456 | tf_op jit(solution)/shard_map/while/body/eval_jaxpr/convert_element_type | solution.py:46
  105.4 4.4 convolution_convert_fusion.3
  109.8 2.5 fusion.39
  113.8 46.7 %all-gather.16.cloned.1.call-done = bf16[768,3072]{1,0:T(8,128)(2,1)} async-done(((bf16[96,3072]{1,0:T(8,128)(2,1)}), bf16[768,3072]{1,0:T(8,128)(2,1)}) %all-gather.16.cloned.1.call-update) | async-done | bytes 4718608 | tf_op jit(solution)/shard_map/all_gather | solution.py:120
  160.4 8.5 %multiply_convert_fusion.1 = (bf16[512,3072]{1,0:T(8,128)(2,1)}, f32[512,3072]{1,0:T(8,128)}) fusion(f32[3072]{0:T(1024)S(1)} %bitcast.111, bf16[768,3072]{1,0:T(8,128)(2,1)} %all-gather.16.cloned.1.call-done, f32[512,768]{1,0:T(8,128)} %copy-done.15, f32[768]{0:T(1024)S(1)} %convert_element_type.234, f32[768]{0:T(1024)S(1)} %convert_element_type.233, ...), kind=kOutput, calls=%fused_computation.15 | convolution fusion | flops 2427322368 | bytes 15751168 | tf_op jit(solution)/shard_map/dot_general | solution.py:171
  169.0 43.5 %all-gather.18.cloned.1.call-done = bf16[3072,768]{1,0:T(8,128)(2,1)} async-done(((bf16[384,768]{1,0:T(8,128)(2,1)}), bf16[3072,768]{1,0:T(8,128)(2,1)}) %all-gather.18.cloned.1.call-update) | async-done | bytes 4718608 | tf_op jit(solution)/shard_map/all_gather | solution.py:122
  212.5 6.2 fusion.40
  222.4 4.9 convert_reduce_fusion
  227.4 3.1 multiply_reduce_fusion.1
  235.9 5.2 convert_reduce_fusion.3
  244.1 3.0 copy.80
  247.2 7.6 %multiply_reduce_fusion = (f32[12,512]{1,0:T(8,128)S(1)}, f32[12,512,512]{1,2,0:T(8,128)S(1)}) fusion(f32[12,512,512]{1,2,0:T(8,128)} %copy-done, f32[12,512]{1,0:T(8,128)S(1)} %log_add_fusion, pred[512]{0:T(512)(128)(4,1)S(1)} %iota_compare_fusion, bf16[512,12,64]{0,2,1:T(8,128)(2,1)} %bitcast.100, bf16[512,12,64]{0,2,1:T(8,128)(2,1)S(1)} %bitcast.96), kind=kOutput, calls=%fused_computation.1 | convolution fusion | flops 418375680 | bytes 26788352 | tf_op jit(solution)/shard_map/while/body/eval_jaxpr/qhd,khd->hqk/dot_general | solution.py:60
  254.8 7.2 %multiply_convert_fusion = bf16[12,512,512]{1,2,0:T(8,128)(2,1)S(1)} fusion(f32[12,512,512]{1,2,0:T(8,128)S(1)} %get-tuple-element.176, f32[12,512,512]{1,2,0:T(8,128)} %copy-done, f32[12,512]{1,0:T(8,128)S(1)} %get-tuple-element.175, f32[12,512]{1,0:T(8,128)S(1)} %log_add_fusion, pred[512]{0:T(512)(128)(4,1)S(1)} %iota_compare_fusion), kind=kLoop, calls=%fused_computation | loop fusion | flops 18874368 | bytes 31506944 | tf_op jit(solution)/shard_map/while/body/eval_jaxpr/convert_element_type | solution.py:64
  267.8 3.1 copy.76
  275.4 4.8 multiply_convert_fusion.2
  283.3 3.1 copy.78
  287.8 7.2 %fusion.33 = f32[768,3072]{1,0:T(8,128)} fusion(bf16[512,3072]{1,0:T(8,128)(2,1)} %copy-done.41, f32[512,768]{1,0:T(8,128)S(1)} %copy-done.18, f32[768]{0:T(1024)S(1)} %convert_element_type.234, f32[768]{0:T(1024)S(1)} %convert_element_type.233, f32[512]{0:T(512)S(1)} %add_rsqrt_fusion.1, f32[512]{0:T(512)S(1)} %broadcast_multiply_fusion.5), kind=kOutput, calls=%fused_computation.91 | convolution fusion | flops 2417885184 | bytes 14166016 | tf_op jit(solution)/shard_map/tr,tc->rc/dot_general | solution.py:83
  296.4 8.2 %fusion.29 = f32[3072,768]{1,0:T(8,128)} fusion(bf16[512,3072]{1,0:T(8,128)(2,1)} %get-tuple-element.170, f32[512,768]{1,0:T(8,128)S(1)} %copy-done.14), kind=kOutput, calls=%fused_computation.87 | convolution fusion | flops 2416312320 | bytes 14155776 | tf_op jit(solution)/shard_map/tr,tc->rc/dot_general | solution.py:83
  306.5 13.8 %reduce-scatter.19.cloned.1.call-done = f32[96,768]{1,0:T(8,128)} async-done(((f32[768,768]{1,0:T(8,128)}), f32[96,768]{1,0:T(8,128)}) %reduce-scatter.19.cloned.1.call-update) | async-done | bytes 294928
  322.0 36.1 %reduce-scatter.13.cloned.1.call-done = f32[96,768]{1,0:T(8,128)} async-done(((f32[768,768]{1,0:T(8,128)}), f32[96,768]{1,0:T(8,128)}) %reduce-scatter.13.cloned.1.call-update) | async-done | bytes 294928 | tf_op jit(solution)/shard_map/reduce_scatter | solution.py:277
  359.8 36.0 %reduce-scatter.21.cloned.1.call-done = f32[96,768]{1,0:T(8,128)} async-done(((f32[768,768]{1,0:T(8,128)}), f32[96,768]{1,0:T(8,128)}) %reduce-scatter.21.cloned.1.call-update) | async-done | bytes 294928
  397.5 99.3 %reduce-scatter.15.cloned.1.call-done = f32[96,3072]{1,0:T(8,128)} async-done(((f32[768,3072]{1,0:T(8,128)}), f32[96,3072]{1,0:T(8,128)}) %reduce-scatter.15.cloned.1.call-update) | async-done | bytes 1179664 | tf_op jit(solution)/shard_map/reduce_scatter | solution.py:281
  499.0 97.9 %reduce-scatter.17.cloned.1.call-done = f32[384,768]{1,0:T(8,128)} async-done(((f32[3072,768]{1,0:T(8,128)}), f32[384,768]{1,0:T(8,128)}) %reduce-scatter.17.cloned.1.call-update) | async-done | bytes 1179664 | tf_op jit(solution)/shard_map/reduce_scatter | solution.py:283
  600.5 26.4 %all-reduce.17 = (bf16[768]{0:T(1024)(128)(2,1)S(1)}, bf16[768]{0:T(1024)(128)(2,1)S(1)}, bf16[768]{0:T(1024)(128)(2,1)S(1)}, bf16[768]{0:T(1024)(128)(2,1)S(1)}...) all-reduce(f32[768]{0:T(1024)S(1)} %reduce_sum.188, ...), channel_id=3, replica_groups=mesh['dp'=4,'fsdp'=8] {'fsdp'}, use_global_device_ids=true, to_apply=%region_14.15.clone | all-reduce | flops 9216 | bytes 55296
  627.6 10.0 %all-reduce.19 = (bf16[96]{0:T(256)(128)(2,1)S(1)}, bf16[96]{0:T(256)(128)(2,1)S(1)}, bf16[96]{0:T(256)(128)(2,1)S(1)}, bf16[96]{0:T(256)(128)(2,1)S(1)}, bf16[9...) all-reduce(bf16[96]{0:T(256)(128)(2,1)S(1)} %dynamic-slice.44, ...), channel_id=1, replica_groups=mesh['dp'=4,'fsdp'=8] {'dp'}, use_global_device_ids=true, to_apply=%region_15.16 | all-reduce | flops 1152 | bytes 4608 | tf_op jit(solution)/shard_map/psum | solution.py:290
  648.1 20.0 %all-reduce.23.cloned.1.call-done = (bf16[96,768]{0,1:T(8,128)(2,1)}, bf16[96,768]{0,1:T(8,128)(2,1)}, bf16[96,768]{0,1:T(8,128)(2,1)}, bf16[96,768]{1,0:T(8,128...) async-done(((bf16[96,768]{0,1:T(8,128)(2,1)}, bf16[96,768]{0,1:T(8,128)(2,1)}, bf16[96,768]{0,1:T(8,128)(2,1)}, bf16[96,768]{1,0:T(8,128)(2,1)}, ...) | async-done | bytes 1769488 | tf_op jit(solution)/shard_map/psum | solution.py:289
  (210 shorter events, 73.8 us)
Async XLA Ops:
  7.2 5.4 copy-start.33
  7.2 5.6 copy-start.34
  7.2 5.8 copy-start.35
  7.2 6.1 copy-start.36
  7.2 6.3 copy-start.37
  7.3 6.5 copy-start.38
  7.3 6.7 copy-start.39
  7.3 7.0 %copy-start.40 = (bf16[96]{0:T(256)(128)(2,1)S(1)}, bf16[96]{0:T(256)(128)(2,1)}, u32[]{:S(2)}) copy-start(bf16[96]{0:T(256)(128)(2,1)} %param.35) | copy-start | bytes 580
  7.3 38.2 %copy-start.29 = (bf16[384]{0:T(512)(128)(2,1)S(1)}, bf16[384]{0:T(512)(128)(2,1)}, u32[]{:S(2)}) copy-start(bf16[384]{0:T(512)(128)(2,1)} %param.31) | copy-start | bytes 2308
  7.3 51.3 %copy-start.4 = (bf16[1,512,768]{2,1,0:T(8,128)(2,1)S(1)}, bf16[1,512,768]{2,1,0:T(8,128)(2,1)}, u32[]{:S(2)}) copy-start(bf16[1,512,768]{2,1,0:T(8,128)(2,1)} %param.18) | copy-start | bytes 2359300
  7.3 51.3 %all-gather.10.cloned.1.call-start = ((), (), s32[]{:S(2)}) async-start(), calls=%async_computation.7 | async-start | bytes 1327104 | tf_op jit(solution)/shard_map/all_gather | solution.py:111
  8.0 53.0 %all-gather.12.cloned.1.call-start = ((), (), s32[]{:S(2)}) async-start(), calls=%async_computation.8 | async-start | bytes 1327104 | tf_op jit(solution)/shard_map/all_gather | solution.py:113
  8.8 74.7 %all-gather.8.cloned.1.call-start = ((), (), s32[]{:S(2)}) async-start(), calls=%async_computation.6 | async-start | bytes 1327104 | tf_op jit(solution)/shard_map/all_gather | solution.py:114
  9.5 100.3 %all-gather.14.cloned.1.call-start = ((), (), s32[]{:S(2)}) async-start(), calls=%async_computation.9 | async-start | bytes 1327104 | tf_op jit(solution)/shard_map/all_gather | solution.py:116
  10.1 150.3 %all-gather.16.cloned.1.call-start = ((), (), s32[]{:S(2)}) async-start(), calls=%async_computation.10 | async-start | bytes 5308416 | tf_op jit(solution)/shard_map/all_gather | solution.py:120
  10.7 201.8 %all-gather.18.cloned.1.call-start = ((), (), s32[]{:S(2)}) async-start(), calls=%async_computation.11 | async-start | bytes 5308416 | tf_op jit(solution)/shard_map/all_gather | solution.py:122
  11.3 293.5 %reduce-scatter.23.cloned.1.call-start = ((), (), s32[]{:S(2)}) async-start(), calls=%async_computation.17 | async-start | bytes 2654208
  61.0 26.9 %copy-start.2 = (bf16[512,768]{0,1:T(8,128)(2,1)}, bf16[512,768]{0,1:T(8,128)(2,1)S(1)}, u32[]{:S(2)}) copy-start(bf16[512,768]{0,1:T(8,128)(2,1)S(1)} %copy.62) | copy-start | bytes 2359300
  90.9 4.5 copy-start
  160.4 52.0 %copy-start.16 = (f32[512,768]{1,0:T(8,128)S(1)}, f32[512,768]{1,0:T(8,128)}, u32[]{:S(2)}) copy-start(f32[512,768]{1,0:T(8,128)} %copy-done.15) | copy-start | bytes 4718596
  212.5 9.9 %copy-start.42 = (f32[512,3072]{1,0:T(8,128)S(1)}, f32[512,3072]{1,0:T(8,128)}, u32[]{:S(2)}) copy-start(f32[512,3072]{1,0:T(8,128)} %get-tuple-element.171) | copy-start | bytes 18874372
  220.7 6.6 slice-start
  222.4 5.0 copy-start.13
  222.4 5.0 slice-start.1
  235.9 6.1 copy-start.5
  247.2 73.1 %reduce-scatter.19.cloned.1.call-start = ((), (), s32[]{:S(2)}) async-start(), calls=%async_computation.15 | async-start | bytes 2654208
  270.9 87.2 %reduce-scatter.13.cloned.1.call-start = ((), (), s32[]{:S(2)}) async-start(), calls=%async_computation.12 | async-start | bytes 2654208 | tf_op jit(solution)/shard_map/reduce_scatter | solution.py:277
  274.3 121.5 %reduce-scatter.21.cloned.1.call-start = ((), (), s32[]{:S(2)}) async-start(), calls=%async_computation.16 | async-start | bytes 2654208
  286.4 210.4 %reduce-scatter.15.cloned.1.call-start = ((), (), s32[]{:S(2)}) async-start(), calls=%async_computation.13 | async-start | bytes 10616832 | tf_op jit(solution)/shard_map/reduce_scatter | solution.py:281
  295.0 301.9 %reduce-scatter.17.cloned.1.call-start = ((), (), s32[]{:S(2)}) async-start(), calls=%async_computation.14 | async-start | bytes 10616832 | tf_op jit(solution)/shard_map/reduce_scatter | solution.py:283
  304.7 363.4 %all-reduce.23.cloned.1.call-start = ((), (), s32[]{:S(2)}) async-start(), calls=%async_computation.18 | async-start | bytes 3833856 | tf_op jit(solution)/shard_map/psum | solution.py:289
  499.0 143.3 %copy-start.12 = (bf16[12,64,512]{2,1,0:T(8,128)(2,1)S(1)}, bf16[12,64,512]{2,1,0:T(8,128)(2,1)}, u32[]{:S(2)}) copy-start(bf16[12,64,512]{2,1,0:T(8,128)(2,1)} %copy-done.11) | copy-start | bytes 2359300
  (26 other events, 56.2 us)
Sparse Core Ops, SparseCore 0:
  9.8 25.5 all-gather.9
  37.0 22.5 all-gather.11
  61.2 22.1 all-gather.7
  85.0 22.4 all-gather.13
  108.9 51.4 all-gather.15
  161.9 50.5 all-gather.17
  247.3 35.0 reduce-scatter.22
  284.7 35.5 reduce-scatter.18
  322.6 35.4 reduce-scatter.12
  360.3 35.4 reduce-scatter.20
  398.1 98.7 reduce-scatter.14
  499.0 97.8 reduce-scatter.16
  601.3 66.7 all-reduce.22
where the time goes:
time: 686 us; the launch traced here: 682 us
  waiting for transfers between devices  417 us (61%)
  matrix products  89.9 us (13%)
  blocking collectives  79.7 us (12%)
  local copies, waits for them, and re-layouts  38.8 us (6%)
  other arithmetic  38.1 us (6%)
  between operations  17.4 us (3%)
    reduce_scatter x1, waiting for transfers between devices, on_device(): lax.psum_scatter(local_grads[9], 'fsdp', scatter_dimension=0, tiled=True)  99.3 us
    reduce_scatter x1, waiting for transfers between devices, on_device(): lax.psum_scatter(local_grads[11], 'fsdp', scatter_dimension=0, tiled=True)  97.9 us
    unnamed x2, blocking collectives  56.7 us
    unnamed x16, waiting for transfers between devices  53.5 us
    all_gather x1, waiting for transfers between devices, on_device(): lax.all_gather(inner_weight, 'fsdp', axis=0, tiled=True)  46.7 us
    all_gather x1, waiting for transfers between devices, on_device(): lax.all_gather(outer_weight, 'fsdp', axis=0, tiled=True)  43.5 us
    reduce_scatter x1, waiting for transfers between devices, on_device(): lax.psum_scatter(local_grads[5], 'fsdp', scatter_dimension=0, tiled=True)  36.1 us
    unnamed x126, local copies, waits for them, and re-layouts  34.3 us
  transfers between devices with their start and end apart: 13, of which 9 were waited for; matrix products, arithmetic and copies ran while one was open for 16% of the time, Pallas kernels for 0%

commit v1 on v0

--- a/solution.py
+++ b/solution.py
@@ -3,6 +3,7 @@
 import jax.numpy as jnp
 from jax import lax
 from jax.sharding import PartitionSpec as P
+from jax.lax import axis_index, axis_size, ppermute
 
 HD = 64
 epsilon = 1e-12
@@ -107,6 +108,25 @@
     second_gain,
     second_shift,
 ):
+
+    def pass_slices(inputs):
+        finding = axis_index("fsdp")
+        later = axis_size("fsdp")
+        tmp, block_next = (later, finding)
+        earlier, v_next = (inputs, 1)
+        while v_next < tmp:
+            column = []
+            s = 0
+            while s < tmp:
+                column.append((s, s ^ v_next))
+                s += 1
+            next_value = ppermute(earlier, "fsdp", column)
+            u1 = jnp.concatenate([earlier, next_value], axis=0)
+            view_out = jnp.concatenate([next_value, earlier], 0)
+            earlier = jnp.where(block_next & v_next == 0, u1, view_out)
+            v_next = 2 * v_next
+        return earlier
+
     gathered = (
         lax.all_gather(query_weight, "fsdp", axis=0, tiled=True),
         lax.all_gather(query_bias, "fsdp", axis=0, tiled=True),
@@ -119,7 +139,7 @@
         lax.all_gather(first_shift, "fsdp", axis=0, tiled=True),
         lax.all_gather(inner_weight, "fsdp", axis=0, tiled=True),
         lax.all_gather(inner_bias, "fsdp", axis=0, tiled=True),
-        lax.all_gather(outer_weight, "fsdp", axis=0, tiled=True),
+        pass_slices(outer_weight),
         lax.all_gather(outer_bias, "fsdp", axis=0, tiled=True),
         lax.all_gather(second_gain, "fsdp", axis=0, tiled=True),
         lax.all_gather(second_shift, "fsdp", axis=0, tiled=True),

time: 686 us -> 781 us (1.14)
  waiting for transfers between devices: 417 us -> 474 us
  blocking collectives: 79.7 us -> 105 us
    all_gather x1, waiting for transfers between devices: 46.7 us -> 93.5 us  [on_device(): lax.all_gather(inner_weight, 'fsdp', axis=0, tiled=True)]
    all_gather x1, waiting for transfers between devices: 0.02 us -> 39.5 us  [on_device(): lax.all_gather(output_weight, 'fsdp', axis=0, tiled=True)]
    unnamed x2, blocking collectives: 56.7 us -> 82.1 us
    all_gather x1, waiting for transfers between devices: 19.9 us -> 0.01 us  [on_device(): lax.all_gather(value_weight, 'fsdp', axis=0, tiled=True)]
    all_gather x1, waiting for transfers between devices: 43.5 us -> 33.1 us  [on_device(): lax.all_gather(outer_weight, 'fsdp', axis=0, tiled=True)]
    unnamed x126 -> x122, local copies, waits for them, and re-layouts: 34.3 us -> 34.4 us
  transfers between devices with their start and end apart: 13 -> 16, of which waited for: 9 -> 10; matrix products, arithmetic and copies ran while one was open for 16% -> 16% of each run, Pallas kernels for 0% -> 0%
where the time goes in v1:
time: 781 us; the launch traced here: 776 us
  waiting for transfers between devices  474 us (61%)
  blocking collectives  105 us (13%)
  matrix products  95.2 us (12%)
  other arithmetic  41.7 us (5%)
  local copies, waits for them, and re-layouts  37.6 us (5%)
  between operations  17.4 us (2%)
    reduce_scatter x1, waiting for transfers between devices, on_device(): lax.psum_scatter(local_grads[9], 'fsdp', scatter_dimension=0, tiled=True)  99.4 us
    reduce_scatter x1, waiting for transfers between devices, on_device(): lax.psum_scatter(local_grads[11], 'fsdp', scatter_dimension=0, tiled=True)  97.9 us
    all_gather x1, waiting for transfers between devices, on_device(): lax.all_gather(inner_weight, 'fsdp', axis=0, tiled=True)  93.5 us
    unnamed x2, blocking collectives  82.1 us
    unnamed x16, waiting for transfers between devices  53 us
    all_gather x1, waiting for transfers between devices, on_device(): lax.all_gather(output_weight, 'fsdp', axis=0, tiled=True)  39.5 us
    reduce_scatter x1, waiting for transfers between devices, on_device(): lax.psum_scatter(local_grads[5], 'fsdp', scatter_dimension=0, tiled=True)  36.1 us
    unnamed x122, local copies, waits for them, and re-layouts  34.4 us
  transfers between devices with their start and end apart: 16, of which 10 were waited for; matrix products, arithmetic and copies ran while one was open for 16% of the time, Pallas kernels for 0%

profile of v1, /device:TPU:0, one launch (start us, length us, event | category | flops | bytes accessed | tf_op | source)
XLA Modules:
  0.0 776.0 jit_solution(16158537936012075230)
XLA Ops:
  13.6 3.0 collective-permute-start.1
  19.8 55.7 %all-reduce.18 = (bf16[768]{0:T(1024)(128)(2,1)S(1)}, bf16[768]{0:T(1024)(128)(2,1)S(1)}, bf16[768]{0:T(1024)(128)(2,1)S(1)}, bf16[768]{0:T(1024)(128)(2,1)S(1)}...) all-reduce(bf16[768]{0:T(1024)(128)(2,1)S(1)} %dynamic-update-slice, ...), channel_id=1, replica_groups=mesh['dp'=4,'fsdp'=8] {'fsdp'}, use_global_device_ids=true, to_apply=%add | all-reduce | flops 6144 | bytes 24576
  76.2 12.7 %all-gather = bf16[8,1,384]{2,1,0:T(2,128)(2,1)S(1)} all-gather(bf16[1,1,384]{2,1,0:T(2,128)(2,1)S(1)} %reshape.181), channel_id=1, replica_groups=mesh['dp'=4,'fsdp'=8] {'fsdp'}, dimensions={0}, use_global_device_ids=true | all-gather | bytes 6912 | tf_op jit(solution)/shard_map/all_gather | solution.py:141
  89.0 3.3 maximum_select_fusion.2
  98.3 3.1 fusion
  101.4 2.6 exponential_reduce_fusion
  105.9 9.8 %fusion.1 = bf16[12,512,512]{1,2,0:T(8,128)(2,1)} fusion(f32[12,512,512]{1,2,0:T(8,128)} %copy-done, f32[12,512]{1,0:T(8,128)S(1)} %log_add_fusion, pred[512]{0:T(512)(128)(4,1)S(1)} %iota_compare_fusion), kind=kLoop, calls=%fused_computation.7 | loop fusion | flops 12582912 | bytes 18899456 | tf_op jit(solution)/shard_map/while/body/eval_jaxpr/convert_element_type | solution.py:47
  118.0 4.1 convolution_convert_fusion.3
  122.2 39.5 %all-gather.14.cloned.1.call-done = bf16[768,768]{1,0:T(8,128)(2,1)} async-done(((bf16[96,768]{1,0:T(8,128)(2,1)}), bf16[768,768]{1,0:T(8,128)(2,1)}) %all-gather.14.cloned.1.call-update) | async-done | bytes 1179664 | tf_op jit(solution)/shard_map/all_gather | solution.py:136
  165.3 93.5 %all-gather.16.cloned.1.call-done = bf16[768,3072]{1,0:T(8,128)(2,1)} async-done(((bf16[96,3072]{1,0:T(8,128)(2,1)}), bf16[768,3072]{1,0:T(8,128)(2,1)}) %all-gather.16.cloned.1.call-update) | async-done | bytes 4718608 | tf_op jit(solution)/shard_map/all_gather | solution.py:140
  258.8 7.6 multiply_convert_fusion.1
  266.3 7.7 fusion.48
  277.7 33.1 %all-gather.18.cloned.1.call-done = bf16[3072,768]{1,0:T(8,128)(2,1)} async-done(((bf16[384,768]{1,0:T(8,128)(2,1)}), bf16[3072,768]{1,0:T(8,128)(2,1)}) %all-gather.18.cloned.1.call-update) | async-done | bytes 4718608 | tf_op jit(solution)/shard_map/all_gather | solution.py:223
  310.8 7.7 convert_reduce_fusion
  318.5 6.6 multiply_reduce_fusion.1
  330.4 5.2 convert_reduce_fusion.3
  338.6 3.0 copy.80
  341.8 7.6 multiply_reduce_fusion
  349.4 7.2 multiply_convert_fusion
  362.3 3.1 copy.76
  369.9 4.8 multiply_convert_fusion.2
  377.8 3.0 copy.78
  382.3 7.2 fusion.41
  390.9 8.2 %fusion.37 = f32[3072,768]{1,0:T(8,128)} fusion(bf16[512,3072]{1,0:T(8,128)(2,1)} %copy-done.19, f32[512,768]{1,0:T(8,128)S(1)} %copy-done.14), kind=kOutput, calls=%fused_computation.98 | convolution fusion | flops 2416312320 | bytes 14155776 | tf_op jit(solution)/shard_map/tr,tc->rc/dot_general | solution.py:84
  401.0 13.7 %reduce-scatter.19.cloned.1.call-done = f32[96,768]{1,0:T(8,128)} async-done(((f32[768,768]{1,0:T(8,128)}), f32[96,768]{1,0:T(8,128)}) %reduce-scatter.19.cloned.1.call-update) | async-done | bytes 294928
  416.5 36.1 %reduce-scatter.13.cloned.1.call-done = f32[96,768]{1,0:T(8,128)} async-done(((f32[768,768]{1,0:T(8,128)}), f32[96,768]{1,0:T(8,128)}) %reduce-scatter.13.cloned.1.call-update) | async-done | bytes 294928 | tf_op jit(solution)/shard_map/reduce_scatter | solution.py:297
  454.2 36.0 %reduce-scatter.21.cloned.1.call-done = f32[96,768]{1,0:T(8,128)} async-done(((f32[768,768]{1,0:T(8,128)}), f32[96,768]{1,0:T(8,128)}) %reduce-scatter.21.cloned.1.call-update) | async-done | bytes 294928
  492.0 99.4 %reduce-scatter.15.cloned.1.call-done = f32[96,3072]{1,0:T(8,128)} async-done(((f32[768,3072]{1,0:T(8,128)}), f32[96,3072]{1,0:T(8,128)}) %reduce-scatter.15.cloned.1.call-update) | async-done | bytes 1179664 | tf_op jit(solution)/shard_map/reduce_scatter | solution.py:301
  593.5 97.9 %reduce-scatter.17.cloned.1.call-done = f32[384,768]{1,0:T(8,128)} async-done(((f32[3072,768]{1,0:T(8,128)}), f32[384,768]{1,0:T(8,128)}) %reduce-scatter.17.cloned.1.call-update) | async-done | bytes 1179664 | tf_op jit(solution)/shard_map/reduce_scatter | solution.py:303
  695.1 26.4 %all-reduce.17 = (bf16[768]{0:T(1024)(128)(2,1)S(1)}, bf16[768]{0:T(1024)(128)(2,1)S(1)}, bf16[768]{0:T(1024)(128)(2,1)S(1)}, bf16[768]{0:T(1024)(128)(2,1)S(1)}...) all-reduce(f32[768]{0:T(1024)S(1)} %reduce_sum.188, ...), channel_id=3, replica_groups=mesh['dp'=4,'fsdp'=8] {'fsdp'}, use_global_device_ids=true, to_apply=%region_14.15.clone | all-reduce | flops 9216 | bytes 55296
  722.2 10.0 %all-reduce.19 = (bf16[96]{0:T(256)(128)(2,1)S(1)}, bf16[96]{0:T(256)(128)(2,1)S(1)}, bf16[96]{0:T(256)(128)(2,1)S(1)}, bf16[96]{0:T(256)(128)(2,1)S(1)}, bf16[9...) all-reduce(bf16[96]{0:T(256)(128)(2,1)S(1)} %dynamic-slice.44, ...), channel_id=1, replica_groups=mesh['dp'=4,'fsdp'=8] {'dp'}, use_global_device_ids=true, to_apply=%region_15.16 | all-reduce | flops 1152 | bytes 4608 | tf_op jit(solution)/shard_map/psum | solution.py:310
  742.7 20.0 %all-reduce.23.cloned.1.call-done = (bf16[96,768]{0,1:T(8,128)(2,1)}, bf16[96,768]{0,1:T(8,128)(2,1)}, bf16[96,768]{0,1:T(8,128)(2,1)}, bf16[96,768]{1,0:T(8,128...) async-done(((bf16[96,768]{0,1:T(8,128)(2,1)}, bf16[96,768]{0,1:T(8,128)(2,1)}, bf16[96,768]{0,1:T(8,128)(2,1)}, bf16[96,768]{1,0:T(8,128)(2,1)}, ...) | async-done | bytes 1769488 | tf_op jit(solution)/shard_map/psum | solution.py:309
  (213 shorter events, 80.1 us)
Async XLA Ops:
  7.2 86.1 %all-gather.10.cloned.1.call-start = ((), (), s32[]{:S(2)}) async-start(), calls=%async_computation.7 | async-start | bytes 1327104 | tf_op jit(solution)/shard_map/all_gather | solution.py:131
  7.9 87.7 %all-gather.12.cloned.1.call-start = ((), (), s32[]{:S(2)}) async-start(), calls=%async_computation.8 | async-start | bytes 1327104 | tf_op jit(solution)/shard_map/all_gather | solution.py:133
  8.7 107.0 %all-gather.8.cloned.1.call-start = ((), (), s32[]{:S(2)}) async-start(), calls=%async_computation.6 | async-start | bytes 1327104 | tf_op jit(solution)/shard_map/all_gather | solution.py:134
  9.4 152.2 %all-gather.14.cloned.1.call-start = ((), (), s32[]{:S(2)}) async-start(), calls=%async_computation.9 | async-start | bytes 1327104 | tf_op jit(solution)/shard_map/all_gather | solution.py:136
  10.0 248.8 %all-gather.16.cloned.1.call-start = ((), (), s32[]{:S(2)}) async-start(), calls=%async_computation.10 | async-start | bytes 5308416 | tf_op jit(solution)/shard_map/all_gather | solution.py:140
  10.6 7.3 copy-start.34
  10.6 7.6 copy-start.35
  10.6 7.8 %copy-start.36 = (bf16[96]{0:T(256)(128)(2,1)S(1)}, bf16[96]{0:T(256)(128)(2,1)}, u32[]{:S(2)}) copy-start(bf16[96]{0:T(256)(128)(2,1)} %param.27) | copy-start | bytes 580
  10.6 8.0 %copy-start.37 = (bf16[96]{0:T(256)(128)(2,1)S(1)}, bf16[96]{0:T(256)(128)(2,1)}, u32[]{:S(2)}) copy-start(bf16[96]{0:T(256)(128)(2,1)} %param.28) | copy-start | bytes 580
  10.6 8.2 %copy-start.38 = (bf16[96]{0:T(256)(128)(2,1)S(1)}, bf16[96]{0:T(256)(128)(2,1)}, u32[]{:S(2)}) copy-start(bf16[96]{0:T(256)(128)(2,1)} %param.29) | copy-start | bytes 580
  10.6 8.5 %copy-start.39 = (bf16[96]{0:T(256)(128)(2,1)S(1)}, bf16[96]{0:T(256)(128)(2,1)}, u32[]{:S(2)}) copy-start(bf16[96]{0:T(256)(128)(2,1)} %param.33) | copy-start | bytes 580
  10.7 8.7 %copy-start.40 = (bf16[96]{0:T(256)(128)(2,1)S(1)}, bf16[96]{0:T(256)(128)(2,1)}, u32[]{:S(2)}) copy-start(bf16[96]{0:T(256)(128)(2,1)} %param.34) | copy-start | bytes 580
  10.7 8.9 %copy-start.41 = (bf16[96]{0:T(256)(128)(2,1)S(1)}, bf16[96]{0:T(256)(128)(2,1)}, u32[]{:S(2)}) copy-start(bf16[96]{0:T(256)(128)(2,1)} %param.35) | copy-start | bytes 580
  10.7 65.5 %copy-start.31 = (bf16[384]{0:T(512)(128)(2,1)S(1)}, bf16[384]{0:T(512)(128)(2,1)}, u32[]{:S(2)}) copy-start(bf16[384]{0:T(512)(128)(2,1)} %param.31) | copy-start | bytes 2308
  10.7 300.1 %all-gather.18.cloned.1.call-start = ((), (), s32[]{:S(2)}) async-start(), calls=%async_computation.11 | async-start | bytes 5308416 | tf_op jit(solution)/shard_map/all_gather | solution.py:223
  10.7 2.4 collective-permute-start
  13.6 75.5 %collective-permute-start.1 = (bf16[768,768]{1,0:T(8,128)(2,1)S(1)}, bf16[768,768]{1,0:T(8,128)(2,1)}, u32[]{:S(2)}, u32[]{:S(2)}) collective-permute-start(bf16[768,768]{1,0:T(8,128)(2,1)S(1)} %maximum_select_fusion.5), channel_id=1, source_target_pairs={{0,2},{1,3},{2,0},{3,1},{4,6},{5,7},{6,4},{7,5},{8,10},{9,11},{10,... | collective-permute-start | bytes 3538952 | tf_op jit(solution)/shard_map/ppermute | solution.py:123
  16.6 382.7 %reduce-scatter.23.cloned.1.call-start = ((), (), s32[]{:S(2)}) async-start(), calls=%async_computation.17 | async-start | bytes 2654208
  92.3 174.1 %collective-permute-start.2 = (bf16[1536,768]{1,0:T(8,128)(2,1)}, bf16[1536,768]{1,0:T(8,128)(2,1)}, u32[]{:S(2)}, u32[]{:S(2)}) collective-permute-start(bf16[1536,768]{1,0:T(8,128)(2,1)} %maximum_select_fusion.2), channel_id=1, source_target_pairs={{0,4},{1,5},{2,6},{3,7},{4,0},{5,1},{6,2},{7,3},{8,12},{9,13},{10,... | collective-permute-start | bytes 7077896 | tf_op jit(solution)/shard_map/ppermute | solution.py:123
  122.2 41.7 %copy-start.9 = (bf16[12,64,512]{2,1,0:T(8,128)(2,1)}, bf16[12,64,512]{2,1,0:T(8,128)(2,1)S(1)}, u32[]{:S(2)}) copy-start(bf16[12,64,512]{2,1,0:T(8,128)(2,1)S(1)} %convolution_convert_fusion.3) | copy-start | bytes 2359300
  258.8 7.6 copy-start.16
  266.3 7.7 copy-start.19
  277.7 40.7 %copy-start.13 = (f32[512,768]{1,0:T(8,128)}, f32[512,768]{1,0:T(8,128)S(1)}, u32[]{:S(2)}) copy-start(f32[512,768]{1,0:T(8,128)S(1)} %get-tuple-element.160) | copy-start | bytes 4718596
  310.8 7.7 copy-start.17
  318.5 6.6 copy-start.42
  341.7 73.0 %reduce-scatter.19.cloned.1.call-start = ((), (), s32[]{:S(2)}) async-start(), calls=%async_computation.15 | async-start | bytes 2654208
  365.4 87.1 %reduce-scatter.13.cloned.1.call-start = ((), (), s32[]{:S(2)}) async-start(), calls=%async_computation.12 | async-start | bytes 2654208 | tf_op jit(solution)/shard_map/reduce_scatter | solution.py:297
  368.8 121.4 %reduce-scatter.21.cloned.1.call-start = ((), (), s32[]{:S(2)}) async-start(), calls=%async_computation.16 | async-start | bytes 2654208
  380.9 210.5 %reduce-scatter.15.cloned.1.call-start = ((), (), s32[]{:S(2)}) async-start(), calls=%async_computation.13 | async-start | bytes 10616832 | tf_op jit(solution)/shard_map/reduce_scatter | solution.py:301
  389.5 301.9 %reduce-scatter.17.cloned.1.call-start = ((), (), s32[]{:S(2)}) async-start(), calls=%async_computation.14 | async-start | bytes 10616832 | tf_op jit(solution)/shard_map/reduce_scatter | solution.py:303
  399.2 363.5 %all-reduce.23.cloned.1.call-start = ((), (), s32[]{:S(2)}) async-start(), calls=%async_computation.18 | async-start | bytes 3833856 | tf_op jit(solution)/shard_map/psum | solution.py:309
  593.5 143.3 %copy-start.12 = (bf16[12,64,512]{2,1,0:T(8,128)(2,1)S(1)}, bf16[12,64,512]{2,1,0:T(8,128)(2,1)}, u32[]{:S(2)}) copy-start(bf16[12,64,512]{2,1,0:T(8,128)(2,1)} %copy-done.11) | copy-start | bytes 2359300
  (27 other events, 70.1 us)
Sparse Core Ops, SparseCore 0:
  9.7 31.6 all-gather.9
  43.0 24.7 all-gather.11
  69.4 22.1 all-gather.7
  93.2 68.4 all-gather.13
  163.1 95.5 all-gather.15
  260.3 50.5 all-gather.17
  341.8 35.3 reduce-scatter.22
  379.6 35.1 reduce-scatter.18
  417.0 35.4 reduce-scatter.12
  454.7 35.4 reduce-scatter.20
  492.6 98.7 reduce-scatter.14
  593.5 97.8 reduce-scatter.16
  695.9 66.7 all-reduce.22
